TPU v7x, 32 devices: a whole 2x2x4 slice. The times are simulated.
32 devices in a mesh: arc: 2 (over y), trow: 4 (over z), tcol: 4 (over x, core).
Axes of the slice: x: 2, y: 2, z: 4, core: 2. Of those that a mesh axis runs over, the one named last changes fastest.
Arguments:
- design: bfloat16 [1280, 8192], P('arc', 'tcol'), may hold values from -0.25 to 0.25
- local_design: bfloat16 [1280, 128], P('arc'), may hold values from -0.3125 to 0.3125
- lengths: int32 [4], P('arc'), may hold values from 1 to 320, 960 in all
- regularizer: float32 [8192], P(('arc', 'trow')), may hold values from 0.2 to 2
Outputs:
- normal: float32 [8192, 8192], P(('arc', 'trow'), 'tcol')
- panel_factor: float32 [2, 8192, 512], P(None, 'tcol')
Inputs may be any that keep to these rules, and one draw needn't show every extreme that they name: `lengths`: each arc has at least one live row; some arc is full.
All inputs are finite; a program needn't handle non-finite values. No bound on the sum of `lengths` on one device may be relied on, other than what follows from the above.
Results may differ from a plain program's by a relative error of at most 0.003.
Values may be sent and summed in bfloat16 or wider, within the bound.
No kernel may reach another device: no remote copies, remote signals or barrier semaphores. Data moves between devices by JAX's collectives and lax.ppermute only.
A program may use at most 128 MiB of HBM per device.

v0:
```python
import jax
import jax.numpy as jnp
from jax import lax
from jax.sharding import PartitionSpec as P

PANEL = 512
PANELS = 2
ridge = 0.1


def broadcast(block, axis, holder):
    block = jnp.where(lax.axis_index(axis) == holder, block, jnp.zeros_like(block))
    return lax.psum(block, axis)


def project_arcs(design, local_design, lengths):
    arc_count = lengths.shape[0]
    row_count = design.shape[0]
    capacity = row_count // arc_count
    arc_blocks = design.reshape(arc_count, capacity, design.shape[1])
    local_half = local_design.reshape(arc_count, capacity, local_design.shape[1])
    live_rows = jnp.arange(capacity, dtype=jnp.int32)[None, :] < lengths[:, None]
    arc_blocks = jnp.where(live_rows[:, :, None], arc_blocks, jnp.zeros((), design.dtype))
    local_half = jnp.where(live_rows[:, :, None], local_half, jnp.zeros((), local_design.dtype))
    local_normal = jnp.einsum(
        "acl,acm->alm", local_half, local_half, preferred_element_type=jnp.float32
    )
    local_normal = local_normal + ridge * jnp.eye(local_half.shape[2], dtype=jnp.float32)[None]
    local_factor = jnp.linalg.cholesky(local_normal)
    local_cols = local_half.astype(jnp.float32)
    basis_rows = lax.linalg.triangular_solve(
        local_factor, jnp.transpose(local_cols, (0, 2, 1)), left_side=True, lower=True
    )
    basis_rows = basis_rows.astype(jnp.bfloat16)
    loadings = jnp.einsum(
        "alc,acw->alw", basis_rows, arc_blocks, preferred_element_type=jnp.float32
    ).astype(jnp.bfloat16)
    cleaned = arc_blocks.astype(jnp.float32) - jnp.einsum(
        "alc,alw->acw", basis_rows, loadings, preferred_element_type=jnp.float32
    )
    return cleaned.astype(jnp.bfloat16).reshape(row_count, design.shape[1])


def contract_rows(left_rows, right_rows):
    return lax.dot_general(
        left_rows, right_rows, (((0,), (0,)), ((), ())), preferred_element_type=jnp.float32
    )


def per_device(design, local_design, lengths, regularizer):
    row_count, col_width = design.shape
    tile_rows = regularizer.shape[0]
    arc_total = lax.axis_size("arc")
    trow_total = lax.axis_size("trow")
    trow_index = lax.axis_index("trow")
    row_start = (lax.axis_index("arc") * trow_total + trow_index) * tile_rows
    col_start = lax.axis_index("tcol") * col_width
    projected = project_arcs(design, local_design, lengths)
    gathered = lax.all_gather(projected, "tcol", axis=1, tiled=True)
    regrouped = gathered.reshape(row_count, arc_total, trow_total, tile_rows)
    selected = lax.dynamic_slice_in_dim(regrouped, trow_index, 1, 2).reshape(
        row_count, arc_total * tile_rows
    )
    received = lax.all_to_all(selected, "arc", split_axis=1, concat_axis=0, tiled=True)
    normal_block = contract_rows(received, lax.all_gather(projected, "arc", axis=0, tiled=True))
    rows_global = row_start + jnp.arange(tile_rows, dtype=jnp.int32)
    cols_global = col_start + jnp.arange(col_width, dtype=jnp.int32)
    on_diagonal = rows_global[:, None] == cols_global[None, :]
    normal_block = normal_block + jnp.where(
        on_diagonal, regularizer[:, None], jnp.zeros((), jnp.float32)
    )
    panel_factors = []
    for panel_index in range(PANELS):
        lead_col = panel_index * PANEL
        padded_rows = jnp.pad(normal_block, ((PANEL, PANEL), (0, 0)))
        slice_start = jnp.clip(lead_col - row_start + PANEL, 0, tile_rows + PANEL)
        slice_rows = lax.dynamic_slice_in_dim(padded_rows, slice_start, PANEL, 0)
        panel_global = lead_col + jnp.arange(PANEL, dtype=jnp.int32)
        in_tile = (panel_global >= row_start) & (panel_global < row_start + tile_rows)
        own_share = jnp.where(in_tile[:, None], slice_rows, jnp.zeros((), jnp.float32))
        panel_strip = lax.psum(own_share, ("arc", "trow"))
        pivot_block, row_strip = (
            broadcast(panel_strip[:, lead_col : lead_col + PANEL], "tcol", 0),
            broadcast(normal_block[:, lead_col : lead_col + PANEL], "tcol", 0),
        )
        lower_factor = jnp.linalg.cholesky(pivot_block)
        col_factor = lax.linalg.triangular_solve(
            lower_factor, panel_strip, left_side=True, lower=True
        ).T
        row_factor = lax.linalg.triangular_solve(
            lower_factor, row_strip.T, left_side=True, lower=True
        ).T
        col_factor = jnp.where(
            cols_global[:, None] >= lead_col, col_factor, jnp.zeros((), jnp.float32)
        )
        row_factor = jnp.where(
            rows_global[:, None] >= lead_col, row_factor, jnp.zeros((), jnp.float32)
        )
        normal_block = normal_block - jnp.dot(
            row_factor, col_factor.T, precision=lax.Precision.HIGHEST
        )
        panel_factors.append(col_factor)
    return (normal_block, jnp.stack(panel_factors))


def solution(mesh):
    return jax.shard_map(
        per_device,
        mesh=mesh,
        in_specs=(P("arc", "tcol"), P("arc", None), P("arc"), P(("arc", "trow"))),
        out_specs=(P(("arc", "trow"), "tcol"), P(None, "tcol", None)),
        check_vma=False,
    )
```

profile of v0, /device:TPU:0, one launch (start us, length us, event | category | flops | bytes accessed | tf_op | source)
XLA Modules:
  0.0 1101.1 jit_solution(17169129062626182126)
XLA Ops:
  9.6 23.5 %custom-call.33 = f32[2,128,128]{2,1,0:T(8,128)S(1)} custom-call(f32[2,128,128]{2,1,0:T(8,128)S(1)} %fusion.105), custom_call_target="Cholesky" | custom-call | tf_op jit(solution)/shard_map/jit(cholesky)/cholesky | solution.py:29
  33.4 19.7 %custom-call.34 = f32[2,1,128,128]{2,3,1,0:T(8,128)S(1)} custom-call(f32[2,1,128,128]{3,2,1,0:T(8,128)S(1)} %select_bitcast_fusion), custom_call_target="InvertDiagBlocksLowerTriangular" | custom-call | tf_op jit(solution)/shard_map/triangular_solve | solution.py:31
  54.3 4.0 subtract_convert_fusion
  58.4 3.0 copy.64
  62.1 72.3 %all-gather.3.cloned.1.call-done = bf16[640,8192]{0,1:T(8,128)(2,1)} async-done(((bf16[640,2048]{0,1:T(8,128)(2,1)}), bf16[640,8192]{0,1:T(8,128)(2,1)}) %all-gather.3.cloned.1.call-update) | async-done | bytes 10485776 | tf_op jit(solution)/shard_map/all_gather | solution.py:59
  136.4 2.6 copy.65
  139.0 3.9 all-to-all-start
  143.5 87.0 %all-gather.5.cloned.1.call-done = bf16[1280,2048]{1,0:T(8,128)(2,1)} async-done(((bf16[640,2048]{1,0:T(8,128)(2,1)}), bf16[1280,2048]{1,0:T(8,128)(2,1)}) %all-gather.5.cloned.1.call-update) | async-done | bytes 5242896 | tf_op jit(solution)/shard_map/all_gather | solution.py:65
  230.4 8.0 select_add_fusion
  238.5 3.4 copy-done.1
  241.9 3.2 fusion
  245.1 3.2 fusion.23
  248.4 152.4 %all-reduce.10.cloned.1.call-done = f32[512,2048]{0,1:T(8,128)} async-done(((f32[512,2048]{0,1:T(8,128)}), f32[512,2048]{0,1:T(8,128)}) %all-reduce.10.cloned.1.call-update) | async-done | bytes 4194320 | tf_op jit(solution)/shard_map/psum | solution.py:81
  403.2 67.9 %all-reduce.16.cloned.1.call-done = (f32[512,512]{0,1:T(8,128)}, f32[512,1024]{1,0:T(8,128)}) async-done(((f32[512,512]{0,1:T(8,128)}, f32[512,1024]{1,0:T(8,128)}), (f32[512,512]{0,1:T(8,128)}, f32[512,1024]{1,0:T(8,128)})) %all-reduce.16.cloned.1.call-update) | async-done | bytes 3145744 | tf_op jit(solution)/shard_map/psum | solution.py:13
  474.1 11.7 %cholesky.327 = f32[128,128]{1,0:T(8,128)S(1)} custom-call(f32[128,128]{1,0:T(8,128)S(1)} %cholesky.467), custom_call_target="Cholesky" | custom-call | tf_op jit(solution)/shard_map/jit(cholesky)/cholesky | solution.py:86
  486.0 9.8 custom-call.40
  496.5 11.7 %cholesky.346 = f32[128,128]{1,0:T(8,128)S(1)} custom-call(f32[128,128]{1,0:T(8,128)S(1)} %cholesky.471), custom_call_target="Cholesky" | custom-call | tf_op jit(solution)/shard_map/jit(cholesky)/cholesky | solution.py:86
  508.2 10.0 custom-call.41
  518.8 11.7 %cholesky.367 = f32[128,128]{1,0:T(8,128)S(1)} custom-call(f32[128,128]{1,0:T(8,128)S(1)} %cholesky.476), custom_call_target="Cholesky" | custom-call | tf_op jit(solution)/shard_map/jit(cholesky)/cholesky | solution.py:86
  530.6 9.8 custom-call.42
  541.0 11.7 %cholesky.384 = f32[128,128]{1,0:T(8,128)S(1)} custom-call(f32[128,128]{1,0:T(8,128)S(1)} %convolution_subtract_fusion.15), custom_call_target="Cholesky" | custom-call | tf_op jit(solution)/shard_map/jit(cholesky)/cholesky | solution.py:86
  558.4 7.7 while.8
  566.2 39.3 %custom-call.43 = f32[4,128,128]{1,2,0:T(8,128)S(1)} custom-call(f32[4,128,128]{2,1,0:T(8,128)S(1)} %get-tuple-element.33), custom_call_target="InvertDiagBlocksLowerTriangular" | custom-call | tf_op jit(solution)/shard_map/triangular_solve/custom-call.9 | solution.py:90
  608.1 3.0 convolution_subtract_fusion.5
  613.6 4.8 convolution_subtract_fusion.3
  623.1 7.3 fusion.17
  639.3 15.1 %convolution_subtract_fusion.1 = f32[1024,2048]{0,1:T(8,128)S(1)} fusion(f32[1024,2048]{0,1:T(8,128)S(1)} %bitcast.164, f32[128,2048]{0,1:T(8,128)S(1)} %fusion.128, f32[128,2048]{0,1:T(8,128)S(1)} %copy-done.4, f32[128,2048]{0,1:T(8,128)S(1)} %copy-done.3, f32[128,2048]{0,1:T(8,128)S(1)} %copy.71, f32[128,1024]{1,0:T(8,128)S(1)} %fusion.129, ...), kind=kOutput, calls=%fused_computation.14 | convolution fusion | flops 12893290496 | bytes 23071744 | tf_op jit(solution)/shard_map/dot_general | solution.py:99
  654.4 3.4 copy-done
  657.8 3.2 fusion.1
  661.1 3.2 fusion.22
  664.2 153.4 %all-reduce.12.cloned.1.call-done = f32[512,2048]{0,1:T(8,128)} async-done(((f32[512,2048]{0,1:T(8,128)}), f32[512,2048]{0,1:T(8,128)}) %all-reduce.12.cloned.1.call-update) | async-done | bytes 4194320 | tf_op jit(solution)/shard_map/psum | solution.py:81
  820.0 3.6 fusion.21
  823.6 64.4 %all-reduce.14.cloned.1.call-done = (f32[512,512]{0,1:T(8,128)}, f32[512,1024]{1,0:T(8,128)}) async-done(((f32[512,512]{0,1:T(8,128)}, f32[512,1024]{1,0:T(8,128)}), (f32[512,512]{0,1:T(8,128)}, f32[512,1024]{1,0:T(8,128)})) %all-reduce.14.cloned.1.call-update) | async-done | bytes 3145744 | tf_op jit(solution)/shard_map/psum | solution.py:13
  891.0 11.7 %cholesky.399 = f32[128,128]{1,0:T(8,128)S(1)} custom-call(f32[128,128]{1,0:T(8,128)S(1)} %cholesky.480), custom_call_target="Cholesky" | custom-call | tf_op jit(solution)/shard_map/jit(cholesky)/cholesky | solution.py:86
  902.9 9.8 custom-call.45
  913.4 11.7 %cholesky.418 = f32[128,128]{1,0:T(8,128)S(1)} custom-call(f32[128,128]{1,0:T(8,128)S(1)} %cholesky.484), custom_call_target="Cholesky" | custom-call | tf_op jit(solution)/shard_map/jit(cholesky)/cholesky | solution.py:86
  925.1 10.0 custom-call.46
  935.8 11.7 %cholesky.439 = f32[128,128]{1,0:T(8,128)S(1)} custom-call(f32[128,128]{1,0:T(8,128)S(1)} %cholesky.489), custom_call_target="Cholesky" | custom-call | tf_op jit(solution)/shard_map/jit(cholesky)/cholesky | solution.py:86
  947.5 9.8 custom-call.47
  957.9 11.7 %cholesky.456 = f32[128,128]{1,0:T(8,128)S(1)} custom-call(f32[128,128]{1,0:T(8,128)S(1)} %convolution_subtract_fusion.14), custom_call_target="Cholesky" | custom-call | tf_op jit(solution)/shard_map/jit(cholesky)/cholesky | solution.py:86
  975.2 8.3 while.9
  983.6 39.3 %custom-call.48 = f32[4,128,128]{1,2,0:T(8,128)S(1)} custom-call(f32[4,128,128]{2,1,0:T(8,128)S(1)} %get-tuple-element.35), custom_call_target="InvertDiagBlocksLowerTriangular" | custom-call | tf_op jit(solution)/shard_map/triangular_solve/custom-call.9 | solution.py:90
  1025.5 3.0 convolution_subtract_fusion.4
  1031.0 4.8 convolution_subtract_fusion.2
  1040.5 7.5 fusion.14
  1060.6 16.5 %convolution_subtract_fusion = f32[1024,2048]{0,1:T(8,128)} fusion(f32[1024,2048]{0,1:T(8,128)S(1)} %bitcast.162, f32[128,2048]{0,1:T(8,128)S(1)} %fusion.134, f32[128,2048]{0,1:T(8,128)S(1)} %copy-done.7, f32[128,2048]{0,1:T(8,128)S(1)} %copy-done.6, f32[128,2048]{0,1:T(8,128)S(1)} %copy.80, f32[128,1024]{1,0:T(8,128)S(1)} %fusion.135, ...), kind=kOutput, calls=%fused_computation.13 | convolution fusion | flops 12893290496 | bytes 23071744 | tf_op jit(solution)/shard_map/dot_general | solution.py:99
  1077.1 9.1 copy.85
  1086.2 7.8 pad_maximum_fusion
  (168 shorter events, 85.0 us)
Async XLA Ops:
  7.2 127.3 %all-gather.3.cloned.1.call-start = ((), (), s32[]{:S(2)}) async-start(), calls=%async_computation.1 | async-start | bytes 13107200 | tf_op jit(solution)/shard_map/all_gather | solution.py:59
  58.4 3.1 copy-start.2
  61.4 169.1 %all-gather.5.cloned.1.call-start = ((), (), s32[]{:S(2)}) async-start(), calls=%async_computation.2 | async-start | bytes 7864320 | tf_op jit(solution)/shard_map/all_gather | solution.py:65
  136.4 94.1 %copy-start.12 = (f32[1024]{0:T(1024)S(1)}, f32[1024]{0:T(1024)}, u32[]{:S(2)}) copy-start(f32[1024]{0:T(1024)} %param.12) | copy-start | bytes 12292
  139.0 91.4 %all-to-all-start = ((bf16[640,2,1024]{2,0,1:T(8,128)(2,1)}), bf16[640,2,1024]{2,0,1:T(8,128)(2,1)S(1)}, u32[]{:S(2)}, u32[]{:S(2)}) async-start(bf16[640,2,1024]{2,0,1:T(8,128)(2,1)} %bitcast.7), calls=%async_computation | async-start | bytes 5242880 | tf_op jit(solution)/shard_map/all_to_all | solution.py:64
  142.9 257.8 %all-reduce.10.cloned.1.call-start = ((), (), s32[]{:S(2)}) async-start(), calls=%async_computation.3 | async-start | bytes 8388608 | tf_op jit(solution)/shard_map/psum | solution.py:81
  238.5 3.4 copy-start.1
  245.1 226.0 %all-reduce.16.cloned.1.call-start = ((), (), s32[]{:S(2)}) async-start(), calls=%async_computation.6 | async-start | bytes 6291456 | tf_op jit(solution)/shard_map/psum | solution.py:13
  403.0 414.6 %all-reduce.12.cloned.1.call-start = ((), (), s32[]{:S(2)}) async-start(), calls=%async_computation.4 | async-start | bytes 8388608 | tf_op jit(solution)/shard_map/psum | solution.py:81
  566.2 42.0 %copy-start.9 = (f32[512,512]{1,0:T(8,128)}, f32[512,512]{1,0:T(8,128)S(1)}, u32[]{:S(2)}) copy-start(f32[512,512]{1,0:T(8,128)S(1)} %get-tuple-element.210) | copy-start | bytes 3145732
  623.1 8.3 copy-start.10
  623.1 16.2 %slice-start.2 = ((s8[8388608]{0:T(1024)(128)(4,1)}), s8[4194304]{0:T(1024)(128)(4,1)S(1)}, s32[]{:S(2)}) async-start(s8[8388608]{0:T(1024)(128)(4,1)} %bitcast.163), calls=%async_computation.9 | async-start | bytes 8388608
  631.4 7.9 copy-start.5
  632.1 7.2 slice-start.3
  633.7 5.7 copy-start.3
  633.7 5.7 copy-start.4
  654.4 3.4 copy-start
  661.0 227.0 %all-reduce.14.cloned.1.call-start = ((), (), s32[]{:S(2)}) async-start(), calls=%async_computation.5 | async-start | bytes 6291456 | tf_op jit(solution)/shard_map/psum | solution.py:13
  983.6 42.0 %copy-start.8 = (f32[512,512]{1,0:T(8,128)}, f32[512,512]{1,0:T(8,128)S(1)}, u32[]{:S(2)}) copy-start(f32[512,512]{1,0:T(8,128)S(1)} %get-tuple-element.209) | copy-start | bytes 3145732
  1040.5 8.6 copy-start.11
  1051.1 5.8 copy-start.6
  1051.1 5.8 copy-start.7
  1051.7 7.5 slice-start
  1056.9 3.7 slice-start.1
Sparse Core Ops, SparseCore 0:
  61.5 72.8 all-gather.2
  136.5 93.8 all-gather.4
  245.2 155.4 all-reduce.9
  403.6 67.4 all-reduce.15
  661.1 156.4 all-reduce.11
  820.5 67.4 all-reduce.13
where the time goes:
time: 1110 us; the launch traced here: 1100 us
  waiting for transfers between devices  598 us (54%)
  other arithmetic  316 us (28%)
  matrix products  109 us (10%)
  local copies, waits for them, and re-layouts  52.6 us (5%)
  between operations  20.3 us (2%)
    psum x2, waiting for transfers between devices, per_device(): panel_strip = lax.psum(own_share, ('arc', 'trow'))  306 us
    another operation x30, other arithmetic, per_device(): lower_factor = jnp.linalg.cholesky(pivot_block)  158 us
    psum x2, waiting for transfers between devices, broadcast(): return lax.psum(block, axis)  132 us
    all_gather x1, waiting for transfers between devices, per_device(): lax.all_gather(projected, 'arc', axis=0, tiled=True)  87 us
    another operation x5, other arithmetic, per_device(): lax.linalg.triangular_solve(lower_factor, row_strip.T, left_side=True, lo...  79.5 us
    all_gather x1, waiting for transfers between devices, per_device(): gathered = lax.all_gather(projected, 'tcol', axis=1, tiled=True)  72.3 us
    another operation x14, matrix products, per_device(): lax.linalg.triangular_solve(lower_factor, panel_strip, left_side=True, lo...  43.5 us
    dot_general x2, matrix products, per_device(): jnp.dot(row_factor, col_factor.T, precision=lax.Precision.HIGHEST)  31.6 us
  transfers between devices with their start and end apart: 7, of which 6 were waited for; matrix products, arithmetic and copies ran while one was open for 1% of the time, Pallas kernels for 0%

commit v1 on v0

--- a/solution.py
+++ b/solution.py
@@ -10,7 +10,7 @@
 
 def broadcast(block, axis, holder):
     block = jnp.where(lax.axis_index(axis) == holder, block, jnp.zeros_like(block))
-    return lax.psum(block, axis)
+    return jnp.sum(lax.all_gather(block, axis), axis=0)
 
 
 def project_arcs(design, local_design, lengths):

time: 1110 us -> 1040 us (0.937)
  waiting for transfers between devices: 598 us -> 529 us
  other arithmetic: 316 us -> 333 us
  matrix products: 109 us -> 95.2 us
    psum x2 -> x0, waiting for transfers between devices: 132 us -> none  [broadcast(): return lax.psum(block, axis)]
    all_gather x0 -> x4, waiting for transfers between devices: none -> 56.5 us  [broadcast(): return jnp.sum(lax.all_gather(block, axis), axis=0)]
    another operation x14, matrix products: 43.5 us -> 25 us  [per_device(): lax.linalg.triangular_solve(lower_factor, panel_strip, left_side=True, lo...]
    reduce_sum x0 -> x4, other arithmetic: none -> 17.5 us  [broadcast(): return jnp.sum(lax.all_gather(block, axis), axis=0)]
  transfers between devices with their start and end apart: 7 -> 9, of which waited for: 6 -> 6; matrix products, arithmetic and copies ran while one was open for 1% -> 32% of each run, Pallas kernels for 0% -> 0%
where the time goes in v1:
time: 1040 us; the launch traced here: 1030 us
  waiting for transfers between devices  529 us (51%)
  other arithmetic  333 us (32%)
  matrix products  95.2 us (9%)
  local copies, waits for them, and re-layouts  49.3 us (5%)
  between operations  20.7 us (2%)
    psum x2, waiting for transfers between devices, per_device(): panel_strip = lax.psum(own_share, ('arc', 'trow'))  312 us
    another operation x30, other arithmetic, per_device(): lower_factor = jnp.linalg.cholesky(pivot_block)  168 us
    all_gather x1, waiting for transfers between devices, per_device(): lax.all_gather(projected, 'arc', axis=0, tiled=True)  87.2 us
    another operation x5, other arithmetic, per_device(): lax.linalg.triangular_solve(lower_factor, row_strip.T, left_side=True, lo...  78.9 us
    all_gather x1, waiting for transfers between devices, per_device(): gathered = lax.all_gather(projected, 'tcol', axis=1, tiled=True)  72.3 us
    all_gather x4, waiting for transfers between devices, broadcast(): return jnp.sum(lax.all_gather(block, axis), axis=0)  56.5 us
    dot_general x2, matrix products, per_device(): jnp.dot(row_factor, col_factor.T, precision=lax.Precision.HIGHEST)  33.9 us
    another operation x14, matrix products, per_device(): lax.linalg.triangular_solve(lower_factor, panel_strip, left_side=True, lo...  25 us
  transfers between devices with their start and end apart: 9, of which 6 were waited for; matrix products, arithmetic and copies ran while one was open for 32% of the time, Pallas kernels for 0%

profile of v1, /device:TPU:0, one launch (start us, length us, event | category | flops | bytes accessed | tf_op | source)
XLA Modules:
  0.0 1031.8 jit_solution(8989303528737078301)
XLA Ops:
  9.6 23.5 %custom-call.33 = f32[2,128,128]{2,1,0:T(8,128)S(1)} custom-call(f32[2,128,128]{2,1,0:T(8,128)S(1)} %fusion.103), custom_call_target="Cholesky" | custom-call | tf_op jit(solution)/shard_map/jit(cholesky)/cholesky | solution.py:29
  33.4 19.7 %custom-call.34 = f32[2,1,128,128]{2,3,1,0:T(8,128)S(1)} custom-call(f32[2,1,128,128]{3,2,1,0:T(8,128)S(1)} %select_bitcast_fusion), custom_call_target="InvertDiagBlocksLowerTriangular" | custom-call | tf_op jit(solution)/shard_map/triangular_solve | solution.py:31
  54.3 4.0 subtract_convert_fusion
  58.4 3.0 copy.34
  62.1 72.3 %all-gather.11.cloned.1.call-done = bf16[640,8192]{0,1:T(8,128)(2,1)} async-done(((bf16[640,2048]{0,1:T(8,128)(2,1)}), bf16[640,8192]{0,1:T(8,128)(2,1)}) %all-gather.11.cloned.1.call-update) | async-done | bytes 10485776 | tf_op jit(solution)/shard_map/all_gather | solution.py:59
  136.4 2.6 copy.35
  139.0 3.9 all-to-all-start
  143.2 87.2 %all-gather.13.cloned.1.call-done = bf16[1280,2048]{1,0:T(8,128)(2,1)} async-done(((bf16[640,2048]{1,0:T(8,128)(2,1)}), bf16[1280,2048]{1,0:T(8,128)(2,1)}) %all-gather.13.cloned.1.call-update) | async-done | bytes 5242896 | tf_op jit(solution)/shard_map/all_gather | solution.py:65
  230.4 7.7 select_add_fusion
  238.2 3.4 copy-done.1
  244.2 155.6 %all-reduce.6.cloned.1.call-done = f32[512,2048]{1,0:T(8,128)} async-done(((f32[512,2048]{1,0:T(8,128)}), f32[512,2048]{1,0:T(8,128)}) %all-reduce.6.cloned.1.call-update) | async-done | bytes 4194320 | tf_op jit(solution)/shard_map/psum | solution.py:81
  402.2 3.1 slice_select_fusion.1
  405.4 30.3 %all-gather.15.cloned.1.call-done = f32[2048,512]{1,0:T(8,128)} async-done(((f32[512,512]{1,0:T(8,128)}), f32[2048,512]{1,0:T(8,128)}) %all-gather.15.cloned.1.call-update) | async-done | bytes 4194320 | tf_op jit(solution)/shard_map/all_gather | solution.py:13
  435.7 2.8 reduce_sum.36
  439.1 11.7 %cholesky.327 = f32[128,128]{1,0:T(8,128)S(1)} custom-call(f32[128,128]{1,0:T(8,128)S(1)} %cholesky.467), custom_call_target="Cholesky" | custom-call | tf_op jit(solution)/shard_map/jit(cholesky)/cholesky | solution.py:86
  450.8 9.8 custom-call.40
  461.4 11.7 %cholesky.346 = f32[128,128]{1,0:T(8,128)S(1)} custom-call(f32[128,128]{1,0:T(8,128)S(1)} %cholesky.471), custom_call_target="Cholesky" | custom-call | tf_op jit(solution)/shard_map/jit(cholesky)/cholesky | solution.py:86
  473.2 18.5 %custom-call.41 = f32[1,128,128]{1,2,0:T(8,128)S(1)} custom-call(f32[1,128,128]{2,1,0:T(8,128)S(1)} %get-tuple-element.83), custom_call_target="InvertDiagBlocksLowerTriangular" | custom-call | tf_op jit(solution)/shard_map/jit(cholesky)/cholesky | solution.py:86
  492.4 11.7 %cholesky.367 = f32[128,128]{1,0:T(8,128)S(1)} custom-call(f32[128,128]{1,0:T(8,128)S(1)} %cholesky.476), custom_call_target="Cholesky" | custom-call | tf_op jit(solution)/shard_map/jit(cholesky)/cholesky | solution.py:86
  504.1 9.8 custom-call.42
  514.6 12.1 %cholesky.384 = f32[128,128]{1,0:T(8,128)S(1)} custom-call(f32[128,128]{1,0:T(8,128)S(1)} %convolution_subtract_fusion.15), custom_call_target="Cholesky" | custom-call | tf_op jit(solution)/shard_map/jit(cholesky)/cholesky | solution.py:86
  532.4 8.4 while.8
  540.8 39.3 %custom-call.43 = f32[4,128,128]{1,2,0:T(8,128)S(1)} custom-call(f32[4,128,128]{2,1,0:T(8,128)S(1)} %get-tuple-element.33), custom_call_target="InvertDiagBlocksLowerTriangular" | custom-call | tf_op jit(solution)/shard_map/triangular_solve/custom-call.9 | solution.py:90
  588.2 2.9 fusion.17
  593.2 6.0 reduce_sum.37
  599.1 3.1 copy.37
  611.4 16.9 %convolution_subtract_fusion.1 = f32[1024,2048]{1,0:T(8,128)S(1)} fusion(f32[1024,2048]{1,0:T(8,128)} %copy-done.1, f32[128,2048]{1,0:T(8,128)S(1)} %copy-done.4, f32[128,2048]{1,0:T(8,128)S(1)} %fusion.124, f32[128,2048]{1,0:T(8,128)S(1)} %fusion.122, f32[128,2048]{1,0:T(8,128)S(1)} %fusion.66, f32[128,1024]{1,0:T(8,128)S(1)} %fusion.127, ...), kind=kOutput, calls=%fused_computation.14 | convolution fusion | flops 12893290496 | bytes 23071744 | tf_op jit(solution)/shard_map/dot_general | solution.py:99
  628.3 3.4 copy-done
  634.4 156.5 %all-reduce.8.cloned.1.call-done = f32[512,2048]{1,0:T(8,128)} async-done(((f32[512,2048]{1,0:T(8,128)}), f32[512,2048]{1,0:T(8,128)}) %all-reduce.8.cloned.1.call-update) | async-done | bytes 4194320 | tf_op jit(solution)/shard_map/psum | solution.py:81
  793.7 3.2 slice_select_fusion
  796.9 3.7 fusion.21
  800.6 26.2 %all-gather.19.cloned.1.call-done = f32[2048,512]{1,0:T(8,128)} async-done(((f32[512,512]{1,0:T(8,128)}), f32[2048,512]{1,0:T(8,128)}) %all-gather.19.cloned.1.call-update) | async-done | bytes 4194320 | tf_op jit(solution)/shard_map/all_gather | solution.py:13
  826.8 2.8 reduce_sum.38
  830.2 11.7 %cholesky.399 = f32[128,128]{1,0:T(8,128)S(1)} custom-call(f32[128,128]{1,0:T(8,128)S(1)} %cholesky.480), custom_call_target="Cholesky" | custom-call | tf_op jit(solution)/shard_map/jit(cholesky)/cholesky | solution.py:86
  841.9 9.8 custom-call.45
  852.5 11.9 %cholesky.418 = f32[128,128]{1,0:T(8,128)S(1)} custom-call(f32[128,128]{1,0:T(8,128)S(1)} %cholesky.484), custom_call_target="Cholesky" | custom-call | tf_op jit(solution)/shard_map/jit(cholesky)/cholesky | solution.py:86
  864.4 9.8 custom-call.46
  874.9 11.7 %cholesky.439 = f32[128,128]{1,0:T(8,128)S(1)} custom-call(f32[128,128]{1,0:T(8,128)S(1)} %cholesky.489), custom_call_target="Cholesky" | custom-call | tf_op jit(solution)/shard_map/jit(cholesky)/cholesky | solution.py:86
  886.7 9.8 custom-call.47
  897.1 11.9 %cholesky.456 = f32[128,128]{1,0:T(8,128)S(1)} custom-call(f32[128,128]{1,0:T(8,128)S(1)} %convolution_subtract_fusion.14), custom_call_target="Cholesky" | custom-call | tf_op jit(solution)/shard_map/jit(cholesky)/cholesky | solution.py:86
  914.3 7.9 while.9
  922.2 39.3 %custom-call.48 = f32[4,128,128]{1,2,0:T(8,128)S(1)} custom-call(f32[4,128,128]{2,1,0:T(8,128)S(1)} %get-tuple-element.35), custom_call_target="InvertDiagBlocksLowerTriangular" | custom-call | tf_op jit(solution)/shard_map/triangular_solve/custom-call.9 | solution.py:90
  969.6 3.0 fusion.14
  976.8 3.8 pad_maximum_fusion
  980.6 8.9 copy.40
  989.5 6.0 reduce_sum.39
  995.5 2.9 copy.39
  1007.6 16.9 %convolution_subtract_fusion = f32[1024,2048]{1,0:T(8,128)} fusion(f32[1024,2048]{1,0:T(8,128)} %copy-done, f32[128,2048]{1,0:T(8,128)S(1)} %copy-done.6, f32[128,2048]{1,0:T(8,128)S(1)} %fusion.130, f32[128,2048]{1,0:T(8,128)S(1)} %fusion.128, f32[128,2048]{1,0:T(8,128)S(1)} %fusion.64, f32[128,1024]{1,0:T(8,128)S(1)} %fusion.133, ...), kind=kOutput, calls=%fused_computation.13 | convolution fusion | flops 12893290496 | bytes 23071744 | tf_op jit(solution)/shard_map/dot_general | solution.py:99
  (166 shorter events, 85.2 us)
Async XLA Ops:
  7.2 127.3 %all-gather.11.cloned.1.call-start = ((), (), s32[]{:S(2)}) async-start(), calls=%async_computation.1 | async-start | bytes 13107200 | tf_op jit(solution)/shard_map/all_gather | solution.py:59
  58.4 3.1 copy-start.3
  61.4 169.1 %all-gather.13.cloned.1.call-start = ((), (), s32[]{:S(2)}) async-start(), calls=%async_computation.2 | async-start | bytes 7864320 | tf_op jit(solution)/shard_map/all_gather | solution.py:65
  136.4 94.1 %copy-start.13 = (f32[1024]{0:T(1024)S(1)}, f32[1024]{0:T(1024)}, u32[]{:S(2)}) copy-start(f32[1024]{0:T(1024)} %param.12) | copy-start | bytes 12292
  139.0 91.4 %all-to-all-start = ((bf16[640,2,1024]{2,0,1:T(8,128)(2,1)}), bf16[640,2,1024]{2,0,1:T(8,128)(2,1)S(1)}, u32[]{:S(2)}, u32[]{:S(2)}) async-start(bf16[640,2,1024]{2,0,1:T(8,128)(2,1)} %bitcast.7), calls=%async_computation | async-start | bytes 5242880 | tf_op jit(solution)/shard_map/all_to_all | solution.py:64
  142.9 256.9 %all-reduce.6.cloned.1.call-start = ((), (), s32[]{:S(2)}) async-start(), calls=%async_computation.3 | async-start | bytes 8388608 | tf_op jit(solution)/shard_map/psum | solution.py:81
  238.1 3.4 copy-start.1
  244.2 191.6 %all-gather.15.cloned.1.call-start = ((), (), s32[]{:S(2)}) async-start(), calls=%async_computation.5 | async-start | bytes 5242880 | tf_op jit(solution)/shard_map/all_gather | solution.py:13
  402.1 191.0 %all-gather.17.cloned.1.call-start = ((), (), s32[]{:S(2)}) async-start(), calls=%async_computation.6 | async-start | bytes 10485760 | tf_op jit(solution)/shard_map/all_gather | solution.py:13
  405.3 385.5 %all-reduce.8.cloned.1.call-start = ((), (), s32[]{:S(2)}) async-start(), calls=%async_computation.4 | async-start | bytes 8388608 | tf_op jit(solution)/shard_map/psum | solution.py:81
  540.8 45.1 %copy-start.12 = (f32[512,512]{1,0:T(8,128)}, f32[512,512]{1,0:T(8,128)S(1)}, u32[]{:S(2)}) copy-start(f32[512,512]{1,0:T(8,128)S(1)} %get-tuple-element.206) | copy-start | bytes 3145732
  580.1 5.7 copy-start.9
  602.2 4.2 copy-start.7
  605.7 5.6 copy-start.4
  628.3 3.4 copy-start
  634.3 192.5 %all-gather.19.cloned.1.call-start = ((), (), s32[]{:S(2)}) async-start(), calls=%async_computation.7 | async-start | bytes 5242880 | tf_op jit(solution)/shard_map/all_gather | solution.py:13
  793.2 196.3 %all-gather.21.cloned.1.call-start = ((), (), s32[]{:S(2)}) async-start(), calls=%async_computation.8 | async-start | bytes 10485760 | tf_op jit(solution)/shard_map/all_gather | solution.py:13
  922.2 45.1 %copy-start.11 = (f32[512,512]{1,0:T(8,128)}, f32[512,512]{1,0:T(8,128)S(1)}, u32[]{:S(2)}) copy-start(f32[512,512]{1,0:T(8,128)S(1)} %get-tuple-element.205) | copy-start | bytes 3145732
  961.5 5.7 copy-start.10
  973.6 1.0 copy-start.5
  974.6 2.2 copy-start.2
  998.5 4.2 copy-start.8
  1002.0 5.6 copy-start.6
Sparse Core Ops, SparseCore 0:
  61.5 72.8 all-gather.10
  136.5 93.8 all-gather.12
  244.3 155.4 all-reduce.5
  402.2 33.4 all-gather.14
  437.7 58.2 all-gather.16
  634.5 156.3 all-reduce.7
  793.3 33.4 all-gather.18
  828.4 58.3 all-gather.20
